TPU v7x, 1024 devices: a whole 4x4x32 slice. The times are simulated.
1024 devices in a mesh: ka: 16 (over y, x), band: 32 (over z), grid: 2 (over core).
Axes of the slice: x: 4, y: 4, z: 32, core: 2. Of those that a mesh axis runs over, the one named last changes fastest.
Arguments:
- target_bands: float32 [16, 1, 2, 32, 1024], P('ka', None, None, 'grid'), may hold values from -6 to 6
- occupied: float32 [16, 32, 2, 32, 1024], P('ka', 'band', None, 'grid'), may hold values from -6 to 6
- qvectors: float32 [8, 3], replicated, may hold values from -1.5 to 1.5
- qmap: int32 [16], replicated, may hold values from 0 to 7
- cutoff: int32 [32, 1024], P('grid'), may hold values 0 or 1
Outputs:
- applied: float32 [16, 1, 2, 32, 1024], P('ka', None, None, 'grid')
All inputs are finite; a program needn't handle non-finite values. No bound on the sum of `cutoff` on one device may be relied on, other than what follows from the above.
Results may differ from a plain program's by a relative error of at most 0.0003.
Values sent between devices are 32-bit elements; how exact they have to be, the bound alone decides.
A program may use at most 32 MiB of HBM per device.

v0:
```python
import math

import jax
import jax.numpy as jnp
from jax import lax
from jax.sharding import PartitionSpec as P

NX = 32
NY = 32
NZ = 32
HOP = 1


SCREEN = 1.0
GSCALE = 0.5


def swapped(value, axis, distance):
    mask = 2**distance
    pairs = [(source, source ^ mask) for source in range(lax.axis_size(axis))]
    return lax.ppermute(value, axis, pairs)


def shifted(value, axis, steps):
    count = lax.axis_size(axis)
    pairs = [(source, (source + steps) % count) for source in range(count)]
    return lax.ppermute(value, axis, pairs)


def dft_tables(length, orient):
    counter = jnp.arange(length, dtype=jnp.int32)
    product = counter[:, None] * counter[None, :] % length
    angles = 2.0 * math.pi / length * product.astype(jnp.float32)
    return (jnp.cos(angles), orient * jnp.sin(angles))


def signed_values(counter, length):
    return jnp.where(counter >= length // 2, counter - length, counter).astype(jnp.float32)


def complex_apply(real_part, imag_part, cos_tab, sin_tab, pattern):
    highest = lax.Precision.HIGHEST
    real_cos = jnp.einsum(pattern, real_part, cos_tab, precision=highest)
    imag_sin = jnp.einsum(pattern, imag_part, sin_tab, precision=highest)
    real_sin = jnp.einsum(pattern, real_part, sin_tab, precision=highest)
    imag_cos = jnp.einsum(pattern, imag_part, cos_tab, precision=highest)
    return (real_cos - imag_sin, real_sin + imag_cos)


def x_transform(real_part, imag_part, orient, slab_pos):
    planes = real_part.shape[1]
    cos_tab, sin_tab = dft_tables(NX, orient)
    start = slab_pos * planes
    other = (1 - slab_pos) * planes
    own_cos = lax.dynamic_slice(cos_tab, (start, start), (planes, planes))
    own_sin = lax.dynamic_slice(sin_tab, (start, start), (planes, planes))
    far_cos = lax.dynamic_slice(cos_tab, (other, start), (planes, planes))
    far_sin = lax.dynamic_slice(sin_tab, (other, start), (planes, planes))
    kept = complex_apply(real_part, imag_part, own_cos, own_sin, "pxyz,wx->pwyz")
    sent = complex_apply(real_part, imag_part, far_cos, far_sin, "pxyz,wx->pwyz")
    arrived = swapped(jnp.stack(sent), "grid", 0)
    return (kept[0] + arrived[0], kept[1] + arrived[1])


def kernel_block(gx_index, gy_index, qvector, keep):
    gx_vals = signed_values(gx_index, NX) * GSCALE + qvector[0]
    gy_vals = signed_values(gy_index, NY) * GSCALE + qvector[1]
    gz_vals = signed_values(jnp.arange(NZ, dtype=jnp.int32), NZ) * GSCALE + qvector[2]
    squares = (
        gx_vals[:, None, None] ** 2 + gy_vals[None, :, None] ** 2 + gz_vals[None, None, :] ** 2
    )
    return 4.0 * math.pi * keep / (squares + SCREEN)


def apply_term(target, orbitals, qvector, cutoff, slab_pos):
    nbands = target.shape[0]
    noccs = orbitals.shape[0]
    planes = target.shape[2]
    shape_grid = (planes, NY, NZ)
    tgt_real = target[:, 0].reshape((nbands, 1) + shape_grid)
    tgt_imag = target[:, 1].reshape((nbands, 1) + shape_grid)
    occ_real = orbitals[:, 0].reshape((1, noccs) + shape_grid)
    occ_imag = orbitals[:, 1].reshape((1, noccs) + shape_grid)
    pair_real = (occ_real * tgt_real + occ_imag * tgt_imag).reshape((-1,) + shape_grid)
    pair_imag = (occ_real * tgt_imag - occ_imag * tgt_real).reshape((-1,) + shape_grid)
    zcos, zsin = dft_tables(NZ, -1.0)
    ycos, ysin = dft_tables(NY, -1.0)
    pair_real, pair_imag = complex_apply(pair_real, pair_imag, zcos, zsin, "pxyz,wz->pxyw")
    pair_real, pair_imag = complex_apply(pair_real, pair_imag, ycos, ysin, "pxyz,wy->pxwz")
    keep_slab = cutoff.reshape(shape_grid).astype(jnp.float32)
    pair_real, pair_imag = x_transform(pair_real, pair_imag, -1.0, slab_pos)
    gx_index = slab_pos * planes + jnp.arange(planes, dtype=jnp.int32)
    kernel = kernel_block(gx_index, jnp.arange(NY, dtype=jnp.int32), qvector, keep_slab)
    pair_real = pair_real * kernel
    pair_imag = pair_imag * kernel
    pair_real, pair_imag = x_transform(pair_real, pair_imag, 1.0, slab_pos)
    zcos_back, zsin_back = dft_tables(NZ, 1.0)
    ycos_back, ysin_back = dft_tables(NY, 1.0)
    pair_real, pair_imag = complex_apply(
        pair_real, pair_imag, ycos_back, ysin_back, "pxyz,wy->pxwz"
    )
    pair_real, pair_imag = complex_apply(
        pair_real, pair_imag, zcos_back, zsin_back, "pxyz,wz->pxyw"
    )
    factor = 1.0 / (NX * NY * NZ)
    pot_real = (pair_real * factor).reshape((nbands, noccs) + shape_grid)
    pot_imag = (pair_imag * factor).reshape((nbands, noccs) + shape_grid)
    out_real = jnp.sum(occ_real * pot_real - occ_imag * pot_imag, axis=1)
    out_imag = jnp.sum(occ_real * pot_imag + occ_imag * pot_real, axis=1)
    return jnp.stack([out_real, out_imag], axis=1).reshape(nbands, 2, planes, NY * NZ)


def pick_qvector(qvectors, qmap, kpoint):
    count = qmap.shape[0]
    chosen_hot = (jnp.arange(count, dtype=jnp.int32) == kpoint).astype(jnp.int32)
    chosen = jnp.sum(chosen_hot * qmap)
    qhot = (jnp.arange(qvectors.shape[0], dtype=jnp.int32) == chosen).astype(jnp.float32)
    return jnp.dot(qhot, qvectors, precision=lax.Precision.HIGHEST)


def shards(target_bands, occupied, qvectors, qmap, cutoff):
    position = lax.axis_index("ka")
    slab_pos = lax.axis_index("grid")
    zero_vector = jnp.zeros((3,), jnp.float32)
    partner = shifted(occupied, "ka", -HOP)
    own_term = apply_term(target_bands[0], occupied[0], zero_vector, cutoff, slab_pos)
    qvector = pick_qvector(qvectors, qmap, position)
    far_term = apply_term(target_bands[0], partner[0], qvector, cutoff, slab_pos)
    combined = -0.5 * (own_term + far_term)
    summed = lax.psum(combined, "band")
    return summed[None]


def solution(mesh):
    return jax.shard_map(
        shards,
        mesh=mesh,
        in_specs=(
            P("ka", None, None, "grid", None),
            P("ka", "band", None, "grid", None),
            P(),
            P(),
            P("grid", None),
        ),
        out_specs=P("ka", None, None, "grid", None),
        check_vma=False,
    )
```

profile of v0, /device:TPU:6, one launch (start us, length us, event | category | flops | bytes accessed | tf_op | source)
XLA Modules:
  0.0 332.8 jit_solution(8920264934849409634)
XLA Ops:
  6.5 2.9 collective-permute-start.2
  9.6 0.8 convert_multiply_fusion
  10.5 0.6 copy-done.3
  11.1 0.6 fusion.228
  11.8 0.8 convolution_bitcast_fusion
  12.5 0.6 fusion.373
  13.2 0.7 add_multiply_fusion.2
  13.8 0.6 add_multiply_fusion.1
  14.6 0.6 add_multiply_fusion
  15.5 0.6 collective-permute-done.2
  17.4 0.4 convolution_subtract_fusion.15
  18.3 0.4 fusion.97
  19.2 0.4 fusion.23
  19.6 0.5 fusion.74
  20.1 0.5 fusion.72
  20.6 0.5 fusion.70
  21.1 0.5 fusion.68
  21.8 0.4 fusion.94
  22.8 0.4 convolution_subtract_fusion.7
  23.7 0.4 fusion.91
  24.5 0.4 fusion.11
  25.0 0.5 fusion.56
  25.5 0.5 fusion.54
  26.0 0.5 fusion.58
  27.0 0.5 fusion.20
  27.5 0.5 fusion.21
  28.0 2.1 collective-permute-start
  30.6 0.5 fusion.9
  31.1 0.5 fusion.8
  31.6 2.4 collective-permute-start.3
  34.0 0.5 fusion.52
  34.6 0.6 fusion.29
  36.9 0.6 fusion.25
  38.8 0.6 fusion.31
  40.3 1.9 collective-permute-start.1
  42.2 0.6 fusion.27
  43.8 2.6 collective-permute-start.4
  47.3 0.5 fusion.38
  47.8 0.5 fusion.40
  48.7 0.5 fusion.16
  50.5 0.5 fusion.32
  51.0 0.5 fusion.34
  51.9 0.5 fusion.4
  53.3 0.5 fusion.14
  54.9 0.5 fusion.2
  56.6 0.7 fusion.77
  57.3 267.0 %all-reduce.2.cloned.1.call-done = f32[1,1,2,16,1024]{4,3,2,1,0:T(8,128)} async-done(((f32[1,1,2,16,1024]{4,3,2,1,0:T(8,128)}), f32[1,1,2,16,1024]{4,3,2,1,0:T(8,128)}) %all-reduce.2.cloned.1.call-update) | async-done | bytes 131088 | tf_op jit(solution)/shard_map/psum | solution.py:130
  324.3 1.6 copy.123
  (68 shorter events, 16.1 us)
Async XLA Ops:
  6.5 5.2 %copy-start = (f32[8,3]{0,1:T(4,128)S(1)}, f32[8,3]{0,1:T(4,128)}, u32[]{:S(2)}) copy-start(f32[8,3]{0,1:T(4,128)} %param.7) | copy-start | bytes 292
  6.5 317.8 %all-reduce.2.cloned.1.call-start = ((), (), s32[]{:S(2)}) async-start(), calls=%async_computation | async-start | bytes 262144 | tf_op jit(solution)/shard_map/psum | solution.py:130
  6.5 9.6 %collective-permute-start.2 = (f32[1,1,2,16,1024]{4,3,2,1,0:T(8,128)}, f32[1,1,2,16,1024]{4,3,2,1,0:T(8,128)S(1)}, u32[]{:S(2)}, u32[]{:S(2)}) collective-permute-start(f32[1,1,2,16,1024]{4,3,2,1,0:T(8,128)} %param.6), channel_id=1, source_target_pairs={{0,960},{64,0},{128,64},{192,128},{256,192},{320,256},{384,320},{4... | collective-permute-start | bytes 393224 | tf_op jit(solution)/shard_map/ppermute | solution.py:27
  10.5 0.7 copy-start.3
  15.3 0.9 copy-start.1
  15.3 1.0 copy-start.2
  28.0 6.5 %collective-permute-start = (f32[2,1,16,32,32]{4,2,3,1,0:T(8,128)S(1)}, f32[2,1,16,32,32]{4,2,3,1,0:T(8,128)S(1)}, u32[]{:S(2)}, u32[]{:S(2)}) collective-permute-start(f32[2,1,16,32,32]{4,2,3,1,0:T(8,128)S(1)} %pad_maximum_fusion), channel_id=1, source_target_pairs={{0,1},{1,0},{2,3},{3,2},{4,5},{5,4},{6,7},{7,6},{8,9},{9,8},{10,11... | collective-permute-start | bytes 393224 | tf_op jit(solution)/shard_map/ppermute | solution.py:21
  31.6 5.3 %collective-permute-start.3 = (f32[2,1,16,32,32]{4,2,3,1,0:T(8,128)S(1)}, f32[2,1,16,32,32]{4,2,3,1,0:T(8,128)S(1)}, u32[]{:S(2)}, u32[]{:S(2)}) collective-permute-start(f32[2,1,16,32,32]{4,2,3,1,0:T(8,128)S(1)} %pad_maximum_fusion.2), channel_id=1, source_target_pairs={{0,1},{1,0},{2,3},{3,2},{4,5},{5,4},{6,7},{7,6},{8,9},{9,8},{10,11... | collective-permute-start | bytes 393224 | tf_op jit(solution)/shard_map/ppermute | solution.py:21
  40.3 6.5 %collective-permute-start.1 = (f32[2,1,16,32,32]{4,2,3,1,0:T(8,128)S(1)}, f32[2,1,16,32,32]{4,2,3,1,0:T(8,128)S(1)}, u32[]{:S(2)}, u32[]{:S(2)}) collective-permute-start(f32[2,1,16,32,32]{4,2,3,1,0:T(8,128)S(1)} %pad_maximum_fusion.1), channel_id=1, source_target_pairs={{0,1},{1,0},{2,3},{3,2},{4,5},{5,4},{6,7},{7,6},{8,9},{9,8},{10,11... | collective-permute-start | bytes 393224 | tf_op jit(solution)/shard_map/ppermute | solution.py:21
  43.8 6.3 %collective-permute-start.4 = (f32[2,1,16,32,32]{4,2,3,1,0:T(8,128)S(1)}, f32[2,1,16,32,32]{4,2,3,1,0:T(8,128)S(1)}, u32[]{:S(2)}, u32[]{:S(2)}) collective-permute-start(f32[2,1,16,32,32]{4,2,3,1,0:T(8,128)S(1)} %pad_maximum_fusion.3), channel_id=1, source_target_pairs={{0,1},{1,0},{2,3},{3,2},{4,5},{5,4},{6,7},{7,6},{8,9},{9,8},{10,11... | collective-permute-start | bytes 393224 | tf_op jit(solution)/shard_map/ppermute | solution.py:21
Sparse Core Ops, SparseCore 0:
  57.4 266.8 all-reduce.1
where the time goes:
time: 333 us
  waiting for transfers between devices  268 us (80%)
  matrix products  30.2 us (9%)
  between operations  14.1 us (4%)
  starting transfers between devices  11.9 us (4%)
  other arithmetic  4.71 us (1%)
  local copies, waits for them, and re-layouts  4.13 us (1%)
    psum x1, waiting for transfers between devices, shards(): summed = lax.psum(combined, 'band')  267 us
    ppermute x4, starting transfers between devices, swapped(): return lax.ppermute(value, axis, pairs)  9.06 us
    dot_general x16, matrix products, complex_apply(): imag_sin = jnp.einsum(pattern, imag_part, sin_tab, precision=highest)  7.5 us
    dot_general x16, matrix products, complex_apply(): imag_cos = jnp.einsum(pattern, imag_part, cos_tab, precision=highest)  7.43 us
    dot_general x16, matrix products, complex_apply(): real_sin = jnp.einsum(pattern, real_part, sin_tab, precision=highest)  7.27 us
    dot_general x16, matrix products, complex_apply(): real_cos = jnp.einsum(pattern, real_part, cos_tab, precision=highest)  7.25 us
  transfers between devices with their start and end apart: 6, of which 2 were waited for; matrix products, arithmetic and copies ran while one was open for 4% of the time, Pallas kernels for 0%

commit v1 on v0

v1 whole, which is shorter than its diff:
```python
import functools
import math

import jax
import jax.numpy as jnp
import ml_dtypes
import numpy as np
from jax import lax
from jax.experimental import pallas as pl
from jax.experimental.pallas import tpu as pltpu
from jax.sharding import PartitionSpec as P

NX = 32
NY = 32
NZ = 32
HOP = 1
SCREEN = 1.0
GSCALE = 0.5

LANES = 128
BLOCKS = NY * NZ // LANES
HALF = NX // 2
GROUPS = 8
NEAR = (4, -4, 3, -3, 2, -2, 1, -1)
MESH = pl.DeviceIdType.MESH


def split_bf16(table):
    table = table.astype(np.float32)
    high = table.astype(ml_dtypes.bfloat16)
    low = (table - high.astype(np.float32)).astype(ml_dtypes.bfloat16)
    return high, low


def make_tables():
    lane = np.arange(LANES)
    low_y, z = lane // NZ, lane % NZ
    phase = np.outer(low_y, low_y) / 4.0 + (np.outer(z, z) % NZ) / NZ
    cos, sin = np.cos(2 * np.pi * phase), np.sin(2 * np.pi * phase)
    forward = np.block([[cos, -sin], [sin, cos]])
    backward = np.block([[cos, sin], [-sin, cos]])
    yz = np.stack([*split_bf16(forward), *split_bf16(backward)])
    x = np.arange(NX)
    angle = 2 * np.pi * (np.outer(x, x) % NX) / NX
    cos, sin = np.cos(angle), np.sin(angle)
    rows = []
    for mat in (np.block([[cos, sin], [-sin, cos]]), np.block([[cos, -sin], [sin, cos]])):
        high, low = split_bf16(mat)
        rows.append(np.concatenate([high, low, high], axis=1))
    turn = 2 * np.pi * np.outer(np.arange(BLOCKS), low_y) / NY
    twiddle = np.concatenate([np.cos(turn), -np.sin(turn)]).astype(np.float32)
    return yz, np.stack(rows), twiddle


def butterflies(real, imag, sign):
    count = len(real)
    if count == 1:
        return real, imag
    even_r, even_i = butterflies(real[::2], imag[::2], sign)
    odd_r, odd_i = butterflies(real[1::2], imag[1::2], sign)
    half = count // 2
    root = math.sqrt(0.5)
    out_r, out_i = [None] * count, [None] * count
    for k in range(half):
        r, i = odd_r[k], odd_i[k]
        turn = k * 8 // count
        if turn == 1:
            r, i = ((r - i) * root, (i + r) * root) if sign > 0 else ((r + i) * root, (i - r) * root)
        elif turn == 2:
            r, i = (-i, r) if sign > 0 else (i, -r)
        elif turn == 3:
            r, i = ((-r - i) * root, (r - i) * root) if sign > 0 else ((i - r) * root, (-i - r) * root)
        out_r[k], out_i[k] = even_r[k] + r, even_i[k] + i
        out_r[k + half], out_i[k + half] = even_r[k] - r, even_i[k] - i
    return out_r, out_i


def halves(value):
    high = value.astype(jnp.bfloat16)
    return high, (value - high.astype(jnp.float32)).astype(jnp.bfloat16)


def mul(a, b):
    return jnp.dot(a, b, preferred_element_type=jnp.float32)


def yz_product(real, imag, high_tab, low_tab):
    rows = jnp.concatenate(
        [jnp.concatenate(real, axis=0), jnp.concatenate(imag, axis=0)], axis=1
    )
    high, low = halves(rows)
    out = mul(high, high_tab) + (mul(low, high_tab) + mul(high, low_tab))
    real = [out[NX * b : NX * (b + 1), :LANES] for b in range(BLOCKS)]
    imag = [out[NX * b : NX * (b + 1), LANES:] for b in range(BLOCKS)]
    return real, imag


def x_product(cols, tab):
    high, low = halves(cols)
    return mul(tab, jnp.concatenate([high, high, low], axis=0))


def pair_potential(rho_r, rho_i, kernel, yz_tab, x_tab, tw_r, tw_i):
    real, imag = butterflies(rho_r, rho_i, -1)
    turned_r = [real[c] * tw_r[c] - imag[c] * tw_i[c] for c in range(BLOCKS)]
    turned_i = [real[c] * tw_i[c] + imag[c] * tw_r[c] for c in range(BLOCKS)]
    real, imag = yz_product(turned_r, turned_i, yz_tab[0], yz_tab[1])
    cols = jnp.concatenate(
        [jnp.concatenate([real[c], imag[c]], axis=0) for c in range(BLOCKS)], axis=1
    )
    spectrum = x_product(cols, x_tab[0])
    weight = jnp.concatenate(kernel, axis=1)
    spectrum = spectrum * jnp.concatenate([weight, weight], axis=0)
    cols = x_product(spectrum, x_tab[1])
    real = [cols[:NX, LANES * c : LANES * (c + 1)] for c in range(BLOCKS)]
    imag = [cols[NX:, LANES * c : LANES * (c + 1)] for c in range(BLOCKS)]
    real, imag = yz_product(real, imag, yz_tab[2], yz_tab[3])
    turned_r = [real[c] * tw_r[c] + imag[c] * tw_i[c] for c in range(BLOCKS)]
    turned_i = [imag[c] * tw_r[c] - real[c] * tw_i[c] for c in range(BLOCKS)]
    return butterflies(turned_r, turned_i, 1)


def signed(index, length):
    return jnp.where(index >= length // 2, index - length, index).astype(jnp.float32)


def screened(block, qx, qy, qz):
    shape = (NX, LANES)
    lane = lax.broadcasted_iota(jnp.int32, shape, 1)
    gx = signed(lax.broadcasted_iota(jnp.int32, shape, 0), NX) * GSCALE + qx
    gy = signed(block + 8 * (lane // NZ), NY) * GSCALE + qy
    gz = signed(lane % NZ, NZ) * GSCALE + qz
    squares = gx * gx + gy * gy + gz * gz
    return (4.0 * math.pi * -0.5 / (NX * NY * NZ)) / (squares + SCREEN)


def reordered(keep, block, roll):
    group = lax.broadcasted_iota(jnp.int32, (NX, LANES), 1) // NZ
    out = None
    for d in range(4):
        source, place = 2 * d + block // 4, block % 4
        piece = roll(keep(source), ((d - place) * NZ) % LANES)
        out = piece if out is None else jnp.where(group == d, piece, out)
    return out


def kernel(
    tgt_in, occ_in, qvectors, qmap, cut_in, yz_tab, x_tab, twiddle,
    out_ref,
    tgt, occ, cut, weight, part, other, summed, near, own, mid, far, total, gathered,
    local_sem, occ_recv, in_send, in_recv, near_send, near_recv, mid_send, mid_recv, back_send, back_recv,
):
    k = lax.axis_index("ka")
    z = lax.axis_index("band")
    core = lax.axis_index("grid")
    far_core = 1 - core
    points = lax.axis_size("ka")
    chips = lax.axis_size("band")

    def chip(delta):
        return lax.rem(z + delta + chips, chips)

    def remote(src, dst, send, recv, where):
        return pltpu.make_async_remote_copy(
            src_ref=src, dst_ref=dst, send_sem=send, recv_sem=recv, device_id=where, device_id_type=MESH
        )

    locals_ = [
        pltpu.make_async_copy(tgt_in.at[0, 0], tgt.at[core], local_sem.at[0]),
        pltpu.make_async_copy(cut_in, cut.at[core], local_sem.at[1]),
    ]
    for copy in locals_:
        copy.start()
    own_occ = pltpu.make_async_copy(occ_in.at[0, 0], occ.at[0], local_sem.at[2])

    @pl.when(core == 0)
    def _():
        own_occ.start()

    barrier = pltpu.get_barrier_semaphore()
    pl.semaphore_signal(barrier, inc=1, device_id={"grid": far_core}, device_id_type=MESH)

    @pl.when(core == 1)
    def _():
        source = lax.rem(k + HOP, points)
        for c in range(2):
            pl.semaphore_signal(barrier, inc=1, device_id={"ka": source, "grid": c}, device_id_type=MESH)

    for delta in NEAR:
        pl.semaphore_signal(barrier, inc=1, device_id={"band": chip(delta)}, device_id_type=MESH)
    pl.semaphore_wait(barrier, 2 + len(NEAR))

    user = lax.rem(k - HOP + points, points)
    sent = [
        remote(occ_in.at[0, 0], occ.at[core], in_send.at[0], occ_recv.at[core], {"ka": user, "grid": 1}),
        remote(tgt_in.at[0, 0], tgt.at[core], in_send.at[1], in_recv.at[1], {"grid": far_core}),
        remote(cut_in, cut.at[core], in_send.at[2], in_recv.at[2], {"grid": far_core}),
    ]
    for copy in sent:
        copy.start()
    cross = remote(occ_in.at[0, 0], occ.at[1], in_send.at[3], occ_recv.at[1], {"grid": 0})

    @pl.when(core == 1)
    def _():
        cross.start()

    chosen = qmap[k]
    used = core.astype(jnp.float32)
    qx, qy, qz = (qvectors[chosen, d] * used for d in range(3))
    for block in range(BLOCKS):
        weight[block] = screened(block, qx, qy, qz)

    locals_[1].wait()
    sent[2].wait_recv()

    def keep(block):
        lanes = slice(LANES * block, LANES * (block + 1))
        return jnp.concatenate([cut[0, :, lanes], cut[1, :, lanes]], axis=0).astype(jnp.float32)

    for block in range(BLOCKS):
        weight[block] = weight[block] * reordered(keep, block, lambda v, s: pltpu.roll(v, s, 1))

    locals_[0].wait()
    sent[1].wait_recv()

    @pl.when(core == 0)
    def _():
        own_occ.wait()
        cross.wait_recv()

    @pl.when(core == 1)
    def _():
        for c in range(2):
            remote(occ_in.at[0, 0], occ.at[c], in_send.at[0], occ_recv.at[c], {"grid": 0}).wait_recv()

    def block_of(ref, which, block):
        lanes = slice(LANES * block, LANES * (block + 1))
        return jnp.concatenate([ref[0, which, :, lanes], ref[1, which, :, lanes]], axis=0)

    rho_r, rho_i = [], []
    for block in range(BLOCKS):
        t_r, t_i = block_of(tgt, 0, block), block_of(tgt, 1, block)
        o_r, o_i = block_of(occ, 0, block), block_of(occ, 1, block)
        rho_r.append(o_r * t_r + o_i * t_i)
        rho_i.append(o_r * t_i - o_i * t_r)
    pot_r, pot_i = pair_potential(
        rho_r,
        rho_i,
        [weight[block] for block in range(BLOCKS)],
        [yz_tab[i] for i in range(4)],
        [x_tab[i] for i in range(2)],
        [twiddle[c : c + 1, :] for c in range(BLOCKS)],
        [twiddle[BLOCKS + c : BLOCKS + c + 1, :] for c in range(BLOCKS)],
    )
    for block in range(BLOCKS):
        o_r, o_i = block_of(occ, 0, block), block_of(occ, 1, block)
        app_r = o_r * pot_r[block] - o_i * pot_i[block]
        app_i = o_r * pot_i[block] + o_i * pot_r[block]
        for half in range(2):
            rows = slice(HALF * half, HALF * (half + 1))
            part[half, block, 0] = app_r[rows]
            part[half, block, 1] = app_i[rows]

    crossing = remote(part.at[far_core], other, in_send.at[4], in_recv.at[4], {"grid": far_core})
    crossing.start()
    crossing.wait_recv()
    summed[...] = part[core] + other[...]

    group = lax.rem(z, GROUPS)

    def pieces(ref, index, delta):
        if abs(delta) < 4:
            return ref.at[index]
        return ref.at[index, 0 if delta > 0 else 1]

    copies = []
    for n, delta in enumerate(NEAR):
        theirs = lax.rem(z + delta + GROUPS, GROUPS)
        slot = 0 if abs(delta) == 4 else n - 1
        copies.append(
            remote(
                pieces(summed, theirs, delta),
                pieces(near, slot, delta),
                near_send.at[n],
                near_recv.at[n],
                {"band": chip(delta)},
            )
        )
        copies[-1].start()
    value = summed[group]
    for copy in copies[::-1]:
        copy.wait_recv()
    for slot in range(len(NEAR) - 1):
        value = value + near[slot]
    own[...] = value

    first = [
        remote(own, mid.at[n], mid_send.at[n], mid_recv.at[n], {"band": chip(delta)})
        for n, delta in enumerate((8, -8))
    ]
    for copy in first:
        copy.start()
    second = [
        remote(mid.at[n, n], far.at[n], mid_send.at[2 + n], mid_recv.at[2 + n], {"band": chip(delta)})
        for n, delta in enumerate((8, -8))
    ]
    for n in range(2):
        first[n].wait_recv()
        second[n].start()
    for copy in second:
        copy.wait_recv()
    value = (own[...] + far[...]) + (mid[0] + mid[1])
    total[...] = value
    gathered[group] = value

    back = []
    for n, delta in enumerate(NEAR):
        source = total if abs(delta) < 4 else total.at[0 if delta > 0 else 1]
        back.append(
            remote(
                source, pieces(gathered, group, delta), back_send.at[n], back_recv.at[n], {"band": chip(delta)}
            )
        )
        back[-1].start()
    for copy in back[::-1]:
        copy.wait_recv()
    for block in range(BLOCKS):
        lanes = slice(LANES * block, LANES * (block + 1))
        for which in range(2):
            out_ref[0, 0, which, :, lanes] = gathered[block, which]

    for copy in [*sent, crossing, *copies, *first, *second, *back]:
        copy.wait_send()

    @pl.when(core == 1)
    def _():
        cross.wait_send()


def shards(target_bands, occupied, qvectors, qmap, cutoff):
    yz_tab, x_tab, twiddle = make_tables()
    f32 = jnp.float32
    planes = (2, HALF, NY * NZ)
    tile = (2, HALF, LANES)
    dma = pltpu.SemaphoreType.DMA
    vmem = pl.BlockSpec(memory_space=pltpu.VMEM)
    smem = pl.BlockSpec(memory_space=pltpu.SMEM)
    anywhere = pl.BlockSpec(memory_space=pl.ANY)
    return pl.pallas_call(
        kernel,
        out_shape=jax.ShapeDtypeStruct(target_bands.shape, f32),
        in_specs=[anywhere, anywhere, smem, smem, anywhere, vmem, vmem, vmem],
        out_specs=vmem,
        scratch_shapes=[
            pltpu.VMEM((2,) + planes, f32),
            pltpu.VMEM((2,) + planes, f32),
            pltpu.VMEM(planes, jnp.int32),
            pltpu.VMEM((BLOCKS, NX, LANES), f32),
            pltpu.VMEM((2, BLOCKS) + tile, f32),
            pltpu.VMEM((BLOCKS,) + tile, f32),
            pltpu.VMEM((BLOCKS,) + tile, f32),
            pltpu.VMEM((len(NEAR) - 1,) + tile, f32),
            pltpu.VMEM(tile, f32),
            pltpu.VMEM((2,) + tile, f32),
            pltpu.VMEM(tile, f32),
            pltpu.VMEM(tile, f32),
            pltpu.VMEM((GROUPS,) + tile, f32),
            dma((3,)),
            dma((2,)),
            dma((5,)),
            dma((5,)),
            dma((len(NEAR),)),
            dma((len(NEAR),)),
            dma((4,)),
            dma((4,)),
            dma((len(NEAR),)),
            dma((len(NEAR),)),
        ],
        compiler_params=pltpu.CompilerParams(collective_id=0, has_side_effects=True),
    )(
        target_bands,
        occupied,
        qvectors,
        qmap,
        cutoff,
        jnp.asarray(yz_tab),
        jnp.asarray(x_tab),
        jnp.asarray(twiddle),
    )


def solution(mesh):
    return jax.shard_map(
        shards,
        mesh=mesh,
        in_specs=(
            P("ka", None, None, "grid", None),
            P("ka", "band", None, "grid", None),
            P(),
            P(),
            P("grid", None),
        ),
        out_specs=P("ka", None, None, "grid", None),
        check_vma=False,
    )
```

time: 333 us -> 58 us (0.17)
  the two profiles are of different devices: /device:TPU:6 before, /device:TPU:30 now
where the time goes in v1:
time: 58 us; the launch traced here: 57.8 us
  Pallas kernels  54.9 us (95%)
  local copies, waits for them, and re-layouts  2.92 us (5%)
    pallas_call x1, Pallas kernels, shards(): pl.pallas_call(kernel, out_shape=jax.ShapeDtypeStruct(target_bands.shape,...  54.9 us
    unnamed x2, local copies, waits for them, and re-layouts  2.92 us

profile of v1, /device:TPU:30, one launch (start us, length us, event | category | flops | bytes accessed | tf_op | source)
XLA Modules:
  0.0 57.8 jit_solution(13194904749328000027)
XLA Ops:
  0.0 1.3 %copy.9.qvectors = f32[8,3]{1,0:T(8,128)} copy(f32[8,3]{0,1:T(4,128)} %param.10) | data formatting | bytes 192 | tf_op args[2]
  1.3 54.9 %shard_map.82 = f32[1,1,2,16,1024]{4,3,2,1,0:T(8,128)} custom-call(f32[1,1,2,16,1024]{4,3,2,1,0:T(8,128)} %tgt_in.1, f32[1,1,2,16,1024]{4,3,2,1,0:T(8,128)} %occ_in.1, f32[8,3]{1,0:T(8,128)} %copy.9.qvectors, s32[16]{0:T(128)} %qmap.1, s32[16,1024]{1,0:T(8,128)} %cut_in.1, bf16[4,256,256]{2,1,0:T(8,128)(2,1)} %constant.6.clone.yz_tab, ...), custom_call_target="tpu_custom_call" | custom-call | tf_op jit(solution)/shard_map/pallas_call | solution.py:349
  56.3 1.6 %copy.11 = f32[1,1,2,16,1024]{4,3,2,1,0:T(8,128)} copy(f32[1,1,2,16,1024]{4,3,2,1,0:T(8,128)} %shard_map.82) | data formatting | bytes 262144

commit v2 on v1

--- a/solution.py
+++ b/solution.py
@@ -145,10 +145,10 @@
 
 
 def kernel(
-    tgt_in, occ_in, qvectors, qmap, cut_in, yz_tab, x_tab, twiddle,
+    tgt_in, occ_in, qvectors, qmap, cut_in, yz_in, x_in, twiddle_in,
     out_ref,
-    tgt, occ, cut, weight, part, other, summed, near, own, mid, far, total, gathered,
-    local_sem, occ_recv, in_send, in_recv, near_send, near_recv, mid_send, mid_recv, back_send, back_recv,
+    yz_tab, x_tab, twiddle, tgt, occ, cut, weight, part, other, summed, near, own, mid, total, gathered,
+    entered, local_sem, occ_recv, in_send, in_recv, near_send, near_recv, mid_send, mid_recv, back_send, back_recv,
 ):
     k = lax.axis_index("ka")
     z = lax.axis_index("band")
@@ -168,7 +168,22 @@
     locals_ = [
         pltpu.make_async_copy(tgt_in.at[0, 0], tgt.at[core], local_sem.at[0]),
         pltpu.make_async_copy(cut_in, cut.at[core], local_sem.at[1]),
+        pltpu.make_async_copy(yz_in, yz_tab, local_sem.at[3]),
+        pltpu.make_async_copy(x_in, x_tab, local_sem.at[4]),
+        pltpu.make_async_copy(twiddle_in, twiddle, local_sem.at[5]),
     ]
+    barrier = pltpu.get_barrier_semaphore()
+    pl.semaphore_signal(barrier, inc=1, device_id={"grid": far_core}, device_id_type=MESH)
+
+    @pl.when(core == 1)
+    def _():
+        source = lax.rem(k + HOP, points)
+        for c in range(2):
+            pl.semaphore_signal(barrier, inc=1, device_id={"ka": source, "grid": c}, device_id_type=MESH)
+
+    for delta in NEAR:
+        pl.semaphore_signal(barrier, inc=1, device_id={"band": chip(delta)}, device_id_type=MESH)
+
     for copy in locals_:
         copy.start()
     own_occ = pltpu.make_async_copy(occ_in.at[0, 0], occ.at[0], local_sem.at[2])
@@ -177,18 +192,14 @@
     def _():
         own_occ.start()
 
-    barrier = pltpu.get_barrier_semaphore()
-    pl.semaphore_signal(barrier, inc=1, device_id={"grid": far_core}, device_id_type=MESH)
-
-    @pl.when(core == 1)
-    def _():
-        source = lax.rem(k + HOP, points)
-        for c in range(2):
-            pl.semaphore_signal(barrier, inc=1, device_id={"ka": source, "grid": c}, device_id_type=MESH)
-
-    for delta in NEAR:
-        pl.semaphore_signal(barrier, inc=1, device_id={"band": chip(delta)}, device_id_type=MESH)
     pl.semaphore_wait(barrier, 2 + len(NEAR))
+
+    def tell(stage):
+        for delta in (4, -4):
+            pl.semaphore_signal(entered.at[stage], inc=1, device_id={"band": chip(delta)}, device_id_type=MESH)
+
+    def hear(stage):
+        pl.semaphore_wait(entered.at[stage], 2)
 
     user = lax.rem(k - HOP + points, points)
     sent = [
@@ -204,9 +215,10 @@
     def _():
         cross.start()
 
+    tell(0)
     chosen = qmap[k]
     used = core.astype(jnp.float32)
-    qx, qy, qz = (qvectors[chosen, d] * used for d in range(3))
+    qx, qy, qz = (qvectors[d, chosen] * used for d in range(3))
     for block in range(BLOCKS):
         weight[block] = screened(block, qx, qy, qz)
 
@@ -220,8 +232,11 @@
     for block in range(BLOCKS):
         weight[block] = weight[block] * reordered(keep, block, lambda v, s: pltpu.roll(v, s, 1))
 
-    locals_[0].wait()
+    for n in (0, 2, 3, 4):
+        locals_[n].wait()
     sent[1].wait_recv()
+    hear(0)
+    tell(1)
 
     @pl.when(core == 0)
     def _():
@@ -294,22 +309,17 @@
         value = value + near[slot]
     own[...] = value
 
-    first = [
+    hear(1)
+    across = [
         remote(own, mid.at[n], mid_send.at[n], mid_recv.at[n], {"band": chip(delta)})
-        for n, delta in enumerate((8, -8))
+        for n, delta in enumerate((12, -12, 4, -4))
     ]
-    for copy in first:
+    for copy in across:
         copy.start()
-    second = [
-        remote(mid.at[n, n], far.at[n], mid_send.at[2 + n], mid_recv.at[2 + n], {"band": chip(delta)})
-        for n, delta in enumerate((8, -8))
-    ]
-    for n in range(2):
-        first[n].wait_recv()
-        second[n].start()
-    for copy in second:
+    for copy in across[::-1]:
         copy.wait_recv()
-    value = (own[...] + far[...]) + (mid[0] + mid[1])
+    value = (mid[0] + mid[3]) + (mid[1] + mid[2])
+    group = lax.rem(z + 4, GROUPS)
     total[...] = value
     gathered[group] = value
 
@@ -329,7 +339,7 @@
         for which in range(2):
             out_ref[0, 0, which, :, lanes] = gathered[block, which]
 
-    for copy in [*sent, crossing, *copies, *first, *second, *back]:
+    for copy in [*sent, crossing, *copies, *across, *back]:
         copy.wait_send()
 
     @pl.when(core == 1)
@@ -349,9 +359,12 @@
     return pl.pallas_call(
         kernel,
         out_shape=jax.ShapeDtypeStruct(target_bands.shape, f32),
-        in_specs=[anywhere, anywhere, smem, smem, anywhere, vmem, vmem, vmem],
+        in_specs=[anywhere, anywhere, smem, smem] + [anywhere] * 4,
         out_specs=vmem,
         scratch_shapes=[
+            pltpu.VMEM(yz_tab.shape, jnp.bfloat16),
+            pltpu.VMEM(x_tab.shape, jnp.bfloat16),
+            pltpu.VMEM(twiddle.shape, f32),
             pltpu.VMEM((2,) + planes, f32),
             pltpu.VMEM((2,) + planes, f32),
             pltpu.VMEM(planes, jnp.int32),
@@ -361,11 +374,11 @@
             pltpu.VMEM((BLOCKS,) + tile, f32),
             pltpu.VMEM((len(NEAR) - 1,) + tile, f32),
             pltpu.VMEM(tile, f32),
-            pltpu.VMEM((2,) + tile, f32),
-            pltpu.VMEM(tile, f32),
+            pltpu.VMEM((4,) + tile, f32),
             pltpu.VMEM(tile, f32),
             pltpu.VMEM((GROUPS,) + tile, f32),
-            dma((3,)),
+            pltpu.SemaphoreType.REGULAR((2,)),
+            dma((6,)),
             dma((2,)),
             dma((5,)),
             dma((5,)),
@@ -380,7 +393,7 @@
     )(
         target_bands,
         occupied,
-        qvectors,
+        qvectors.T,
         qmap,
         cutoff,
         jnp.asarray(yz_tab),

time: 58 us -> 50.8 us (0.88)
  the two profiles are of different devices: /device:TPU:30 before, /device:TPU:6 now
where the time goes in v2:
time: 50.8 us; the launch traced here: 50 us
  Pallas kernels  48.4 us (95%)
  local copies, waits for them, and re-layouts  1.57 us (3%)
    pallas_call x1, Pallas kernels, shards(): pl.pallas_call(kernel, out_shape=jax.ShapeDtypeStruct(target_bands.shape,...  48.4 us
    unnamed x1, local copies, waits for them, and re-layouts  1.57 us

profile of v2, /device:TPU:6, one launch (start us, length us, event | category | flops | bytes accessed | tf_op | source)
XLA Modules:
  0.0 50.0 jit_solution(1788228962011111790)
XLA Ops:
  0.0 48.4 %shard_map.82 = f32[1,1,2,16,1024]{4,3,2,1,0:T(8,128)} custom-call(f32[1,1,2,16,1024]{4,3,2,1,0:T(8,128)} %tgt_in.1, f32[1,1,2,16,1024]{4,3,2,1,0:T(8,128)} %occ_in.1, f32[3,8]{1,0:T(4,128)} %bitcast.1, s32[16]{0:T(128)} %qmap.1, s32[16,1024]{1,0:T(8,128)} %cut_in.1, bf16[4,256,256]{2,1,0:T(8,128)(2,1)} %constant.6.clone.yz_in, ...), custom_call_target="tpu_custom_call" | custom-call | tf_op jit(solution)/shard_map/pallas_call | solution.py:359
  48.5 1.6 %copy.10 = f32[1,1,2,16,1024]{4,3,2,1,0:T(8,128)} copy(f32[1,1,2,16,1024]{4,3,2,1,0:T(8,128)} %shard_map.82) | data formatting | bytes 262144

commit v3 on v2

--- a/solution.py
+++ b/solution.py
@@ -145,9 +145,9 @@
 
 
 def kernel(
-    tgt_in, occ_in, qvectors, qmap, cut_in, yz_in, x_in, twiddle_in,
+    tgt_in, occ_in, qvectors_in, qmap_in, cut_in, yz_in, x_in, twiddle_in,
     out_ref,
-    yz_tab, x_tab, twiddle, tgt, occ, cut, weight, part, other, summed, near, own, mid, total, gathered,
+    qvectors, qmap, yz_tab, x_tab, twiddle, tgt, occ, cut, weight, part, other, summed, near, own, mid, total, gathered,
     entered, local_sem, occ_recv, in_send, in_recv, near_send, near_recv, mid_send, mid_recv, back_send, back_recv,
 ):
     k = lax.axis_index("ka")
@@ -171,6 +171,8 @@
         pltpu.make_async_copy(yz_in, yz_tab, local_sem.at[3]),
         pltpu.make_async_copy(x_in, x_tab, local_sem.at[4]),
         pltpu.make_async_copy(twiddle_in, twiddle, local_sem.at[5]),
+        pltpu.make_async_copy(qvectors_in, qvectors, local_sem.at[6]),
+        pltpu.make_async_copy(qmap_in, qmap, local_sem.at[7]),
     ]
     barrier = pltpu.get_barrier_semaphore()
     pl.semaphore_signal(barrier, inc=1, device_id={"grid": far_core}, device_id_type=MESH)
@@ -216,6 +218,8 @@
         cross.start()
 
     tell(0)
+    for n in (5, 6):
+        locals_[n].wait()
     chosen = qmap[k]
     used = core.astype(jnp.float32)
     qx, qy, qz = (qvectors[d, chosen] * used for d in range(3))
@@ -354,14 +358,15 @@
     tile = (2, HALF, LANES)
     dma = pltpu.SemaphoreType.DMA
     vmem = pl.BlockSpec(memory_space=pltpu.VMEM)
-    smem = pl.BlockSpec(memory_space=pltpu.SMEM)
     anywhere = pl.BlockSpec(memory_space=pl.ANY)
     return pl.pallas_call(
         kernel,
-        out_shape=jax.ShapeDtypeStruct(target_bands.shape, f32),
-        in_specs=[anywhere, anywhere, smem, smem] + [anywhere] * 4,
+        out_shape=pltpu.VMEM(target_bands.shape, f32),
+        in_specs=[anywhere] * 8,
         out_specs=vmem,
         scratch_shapes=[
+            pltpu.SMEM(qvectors.shape[::-1], f32),
+            pltpu.SMEM(qmap.shape, jnp.int32),
             pltpu.VMEM(yz_tab.shape, jnp.bfloat16),
             pltpu.VMEM(x_tab.shape, jnp.bfloat16),
             pltpu.VMEM(twiddle.shape, f32),
@@ -378,7 +383,7 @@
             pltpu.VMEM(tile, f32),
             pltpu.VMEM((GROUPS,) + tile, f32),
             pltpu.SemaphoreType.REGULAR((2,)),
-            dma((6,)),
+            dma((8,)),
             dma((2,)),
             dma((5,)),
             dma((5,)),
@@ -389,16 +394,12 @@
             dma((len(NEAR),)),
             dma((len(NEAR),)),
         ],
-        compiler_params=pltpu.CompilerParams(collective_id=0, has_side_effects=True),
+        compiler_params=pltpu.CompilerParams(collective_id=0, has_side_effects=True, vmem_limit_bytes=24 * 2**20),
     )(
-        target_bands,
-        occupied,
-        qvectors.T,
-        qmap,
-        cutoff,
-        jnp.asarray(yz_tab),
-        jnp.asarray(x_tab),
-        jnp.asarray(twiddle),
+        *(
+            pltpu.with_memory_space_constraint(value, pltpu.HBM)
+            for value in (target_bands, occupied, qvectors.T, qmap, cutoff, *map(jnp.asarray, (yz_tab, x_tab, twiddle)))
+        )
     )
 
 

time: 50.8 us -> 48.5 us (0.955)
  Pallas kernels: 48.4 us -> 47.1 us
  local copies, waits for them, and re-layouts: 1.57 us -> 0.66 us
    pallas_call x1, Pallas kernels: 48.4 us -> 47.1 us  [shards(): pl.pallas_call(kernel, out_shape=pltpu.VMEM(target_bands.shape, f32), in_...]
    unnamed x1, local copies, waits for them, and re-layouts: 1.57 us -> 0.66 us
where the time goes in v3:
time: 48.5 us; the launch traced here: 47.8 us
  Pallas kernels  47.1 us (97%)
  local copies, waits for them, and re-layouts  0.66 us (1%)
    pallas_call x1, Pallas kernels, shards(): pl.pallas_call(kernel, out_shape=pltpu.VMEM(target_bands.shape, f32), in_...  47.1 us

profile of v3, /device:TPU:6, one launch (start us, length us, event | category | flops | bytes accessed | tf_op | source)
XLA Modules:
  0.0 47.8 jit_solution(12055020658302176150)
XLA Ops:
  0.0 47.1 %shard_map.82 = f32[1,1,2,16,1024]{4,3,2,1,0:T(8,128)S(1)} custom-call(f32[1,1,2,16,1024]{4,3,2,1,0:T(8,128)} %tgt_in.1, f32[1,1,2,16,1024]{4,3,2,1,0:T(8,128)} %occ_in.1, f32[3,8]{1,0:T(4,128)} %bitcast.1, s32[16]{0:T(128)} %qmap_in.1, s32[16,1024]{1,0:T(8,128)} %cut_in.1, bf16[4,256,256]{2,1,0:T(8,128)(2,1)} %constant.6.clone.yz_in, ...), custom_call_target="tpu_custom_call" | custom-call | tf_op jit(solution)/shard_map/pallas_call | solution.py:362
  47.1 0.7 %copy.10 = f32[1,1,2,16,1024]{4,3,2,1,0:T(8,128)} copy(f32[1,1,2,16,1024]{4,3,2,1,0:T(8,128)S(1)} %shard_map.82) | data formatting | bytes 262144

commit v4 on v3

--- a/solution.py
+++ b/solution.py
@@ -90,8 +90,9 @@
     )
     high, low = halves(rows)
     out = mul(high, high_tab) + (mul(low, high_tab) + mul(high, low_tab))
-    real = [out[NX * b : NX * (b + 1), :LANES] for b in range(BLOCKS)]
-    imag = [out[NX * b : NX * (b + 1), LANES:] for b in range(BLOCKS)]
+    count = real[0].shape[0]
+    real = [out[count * b : count * (b + 1), :LANES] for b in range(BLOCKS)]
+    imag = [out[count * b : count * (b + 1), LANES:] for b in range(BLOCKS)]
     return real, imag
 
 
@@ -100,7 +101,7 @@
     return mul(tab, jnp.concatenate([high, high, low], axis=0))
 
 
-def pair_potential(rho_r, rho_i, kernel, yz_tab, x_tab, tw_r, tw_i):
+def screened_spectrum(rho_r, rho_i, kernel, yz_tab, x_tab, tw_r, tw_i):
     real, imag = butterflies(rho_r, rho_i, -1)
     turned_r = [real[c] * tw_r[c] - imag[c] * tw_i[c] for c in range(BLOCKS)]
     turned_i = [real[c] * tw_i[c] + imag[c] * tw_r[c] for c in range(BLOCKS)]
@@ -114,6 +115,10 @@
     cols = x_product(spectrum, x_tab[1])
     real = [cols[:NX, LANES * c : LANES * (c + 1)] for c in range(BLOCKS)]
     imag = [cols[NX:, LANES * c : LANES * (c + 1)] for c in range(BLOCKS)]
+    return real, imag
+
+
+def back_along_yz(real, imag, yz_tab, tw_r, tw_i):
     real, imag = yz_product(real, imag, yz_tab[2], yz_tab[3])
     turned_r = [real[c] * tw_r[c] + imag[c] * tw_i[c] for c in range(BLOCKS)]
     turned_i = [imag[c] * tw_r[c] - real[c] * tw_i[c] for c in range(BLOCKS)]
@@ -209,6 +214,7 @@
         remote(tgt_in.at[0, 0], tgt.at[core], in_send.at[1], in_recv.at[1], {"grid": far_core}),
         remote(cut_in, cut.at[core], in_send.at[2], in_recv.at[2], {"grid": far_core}),
     ]
+    tell(0)
     for copy in sent:
         copy.start()
     cross = remote(occ_in.at[0, 0], occ.at[1], in_send.at[3], occ_recv.at[1], {"grid": 0})
@@ -217,7 +223,6 @@
     def _():
         cross.start()
 
-    tell(0)
     for n in (5, 6):
         locals_[n].wait()
     chosen = qmap[k]
@@ -262,28 +267,43 @@
         o_r, o_i = block_of(occ, 0, block), block_of(occ, 1, block)
         rho_r.append(o_r * t_r + o_i * t_i)
         rho_i.append(o_r * t_i - o_i * t_r)
-    pot_r, pot_i = pair_potential(
+    tables = [yz_tab[i] for i in range(4)]
+    tw_r = [twiddle[c : c + 1, :] for c in range(BLOCKS)]
+    tw_i = [twiddle[BLOCKS + c : BLOCKS + c + 1, :] for c in range(BLOCKS)]
+    real, imag = screened_spectrum(
         rho_r,
         rho_i,
         [weight[block] for block in range(BLOCKS)],
-        [yz_tab[i] for i in range(4)],
+        tables,
         [x_tab[i] for i in range(2)],
-        [twiddle[c : c + 1, :] for c in range(BLOCKS)],
-        [twiddle[BLOCKS + c : BLOCKS + c + 1, :] for c in range(BLOCKS)],
+        tw_r,
+        tw_i,
     )
-    for block in range(BLOCKS):
-        o_r, o_i = block_of(occ, 0, block), block_of(occ, 1, block)
-        app_r = o_r * pot_r[block] - o_i * pot_i[block]
-        app_i = o_r * pot_i[block] + o_i * pot_r[block]
-        for half in range(2):
-            rows = slice(HALF * half, HALF * (half + 1))
-            part[half, block, 0] = app_r[rows]
-            part[half, block, 1] = app_i[rows]
-
-    crossing = remote(part.at[far_core], other, in_send.at[4], in_recv.at[4], {"grid": far_core})
-    crossing.start()
-    crossing.wait_recv()
-    summed[...] = part[core] + other[...]
+
+    crossings = []
+    for n in range(4):
+        where = pl.ds(2 * n, 2)
+        crossings.append(
+            remote(part.at[far_core, where], other.at[where], in_send.at[4 + n], in_recv.at[4 + n], {"grid": far_core})
+        )
+
+    def send():
+        for copy in crossings:
+            copy.start()
+
+    for half in range(2):
+        rows = slice(HALF * half, HALF * (half + 1))
+        pot_r, pot_i = back_along_yz([r[rows] for r in real], [i[rows] for i in imag], tables, tw_r, tw_i)
+        for block in range(BLOCKS):
+            lanes = slice(LANES * block, LANES * (block + 1))
+            o_r, o_i = occ[half, 0, :, lanes], occ[half, 1, :, lanes]
+            part[half, block, 0] = o_r * pot_r[block] - o_i * pot_i[block]
+            part[half, block, 1] = o_r * pot_i[block] + o_i * pot_r[block]
+        pl.when(core == 1 - half)(send)
+    for n, copy in enumerate(crossings):
+        copy.wait_recv()
+        where = slice(2 * n, 2 * n + 2)
+        summed[where] = part[core, where] + other[where]
 
     group = lax.rem(z, GROUPS)
 
@@ -343,7 +363,7 @@
         for which in range(2):
             out_ref[0, 0, which, :, lanes] = gathered[block, which]
 
-    for copy in [*sent, crossing, *copies, *across, *back]:
+    for copy in [*sent, *crossings, *copies, *across, *back]:
         copy.wait_send()
 
     @pl.when(core == 1)
@@ -385,8 +405,8 @@
             pltpu.SemaphoreType.REGULAR((2,)),
             dma((8,)),
             dma((2,)),
-            dma((5,)),
-            dma((5,)),
+            dma((8,)),
+            dma((8,)),
             dma((len(NEAR),)),
             dma((len(NEAR),)),
             dma((4,)),

time: 48.5 us -> 48.5 us (level)
  no operation moved by 1% of the time
where the time goes in v4:
time: 48.5 us; the launch traced here: 48 us
  Pallas kernels  47.3 us (98%)
  local copies, waits for them, and re-layouts  0.66 us (1%)
    pallas_call x1, Pallas kernels, shards(): pl.pallas_call(kernel, out_shape=pltpu.VMEM(target_bands.shape, f32), in_...  47.3 us

profile of v4, /device:TPU:6, one launch (start us, length us, event | category | flops | bytes accessed | tf_op | source)
XLA Modules:
  0.0 48.0 jit_solution(8472802640499705098)
XLA Ops:
  0.0 47.3 %shard_map.82 = f32[1,1,2,16,1024]{4,3,2,1,0:T(8,128)S(1)} custom-call(f32[1,1,2,16,1024]{4,3,2,1,0:T(8,128)} %tgt_in.1, f32[1,1,2,16,1024]{4,3,2,1,0:T(8,128)} %occ_in.1, f32[3,8]{1,0:T(4,128)} %bitcast.1, s32[16]{0:T(128)} %qmap_in.1, s32[16,1024]{1,0:T(8,128)} %cut_in.1, bf16[4,256,256]{2,1,0:T(8,128)(2,1)} %constant.6.clone.yz_in, ...), custom_call_target="tpu_custom_call" | custom-call | tf_op jit(solution)/shard_map/pallas_call | solution.py:382
  47.3 0.7 %copy.10 = f32[1,1,2,16,1024]{4,3,2,1,0:T(8,128)} copy(f32[1,1,2,16,1024]{4,3,2,1,0:T(8,128)S(1)} %shard_map.82) | data formatting | bytes 262144

commit v5 on v3

--- a/solution.py
+++ b/solution.py
@@ -307,10 +307,12 @@
         )
         copies[-1].start()
     value = summed[group]
-    for copy in copies[::-1]:
+    for n in range(len(NEAR) - 1, 1, -1):
+        copies[n].wait_recv()
+        value = value + near[n - 1]
+    for copy in copies[:2]:
         copy.wait_recv()
-    for slot in range(len(NEAR) - 1):
-        value = value + near[slot]
+    value = value + near[0]
     own[...] = value
 
     hear(1)
@@ -336,12 +338,18 @@
             )
         )
         back[-1].start()
-    for copy in back[::-1]:
+    def put(index):
+        lanes = pl.ds(pl.multiple_of(index * LANES, LANES), LANES)
+        for which in range(2):
+            out_ref[0, 0, which, :, lanes] = gathered[index, which]
+
+    put(group)
+    for n in range(len(NEAR) - 1, 1, -1):
+        back[n].wait_recv()
+        put(lax.rem(group - NEAR[n] + GROUPS, GROUPS))
+    for copy in back[:2]:
         copy.wait_recv()
-    for block in range(BLOCKS):
-        lanes = slice(LANES * block, LANES * (block + 1))
-        for which in range(2):
-            out_ref[0, 0, which, :, lanes] = gathered[block, which]
+    put(lax.rem(group + 4, GROUPS))
 
     for copy in [*sent, crossing, *copies, *across, *back]:
         copy.wait_send()

time: 48.5 us -> 48.5 us (level)
  no operation moved by 1% of the time
where the time goes in v5:
time: 48.5 us; the launch traced here: 47.8 us
  Pallas kernels  47.1 us (97%)
  local copies, waits for them, and re-layouts  0.66 us (1%)
    pallas_call x1, Pallas kernels, shards(): pl.pallas_call(kernel, out_shape=pltpu.VMEM(target_bands.shape, f32), in_...  47.1 us

profile of v5, /device:TPU:6, one launch (start us, length us, event | category | flops | bytes accessed | tf_op | source)
XLA Modules:
  0.0 47.8 jit_solution(6807100845772859882)
XLA Ops:
  0.0 47.1 %shard_map.82 = f32[1,1,2,16,1024]{4,3,2,1,0:T(8,128)S(1)} custom-call(f32[1,1,2,16,1024]{4,3,2,1,0:T(8,128)} %tgt_in.1, f32[1,1,2,16,1024]{4,3,2,1,0:T(8,128)} %occ_in.1, f32[3,8]{1,0:T(4,128)} %bitcast.1, s32[16]{0:T(128)} %qmap_in.1, s32[16,1024]{1,0:T(8,128)} %cut_in.1, bf16[4,256,256]{2,1,0:T(8,128)(2,1)} %constant.6.clone.yz_in, ...), custom_call_target="tpu_custom_call" | custom-call | tf_op jit(solution)/shard_map/pallas_call | solution.py:370
  47.1 0.7 %copy.10 = f32[1,1,2,16,1024]{4,3,2,1,0:T(8,128)} copy(f32[1,1,2,16,1024]{4,3,2,1,0:T(8,128)S(1)} %shard_map.82) | data formatting | bytes 262144
